TPU v7x, 512 devices: a whole 4x4x16 slice. The times are simulated.
512 devices in a mesh: seq: 32 (over z, core), img: 16 (over y, x).
Axes of the slice: x: 4, y: 4, z: 16, core: 2. Of those that a mesh axis runs over, the one named last changes fastest.
Arguments:
- tokens: bfloat16 [16, 96, 128, 2240], P('img', 'seq'), may hold values from -8 to 8
- norm_gain: bfloat16 [2240], replicated, may hold values from 0.099609375 to 1.8984375
- caption: bfloat16 [16, 2240], P('img'), may hold values from -6 to 6
- null_caption: bfloat16 [2240], replicated, may hold values from -6 to 6
- keep: int32 [16], P('img'), may hold values from 0 to 1, as said below
- bucket_rows: int32 [16], P('img'), may hold values from 25 to 96, as said below
- w_qkv: bfloat16 [2240, 3456], P('img', 'seq'), may hold values from -0.125 to 0.125
Outputs:
- attended: bfloat16 [16, 96, 128, 1152], P('img', 'seq')
Inputs may be any that keep to these rules, and one draw needn't show every extreme that they name: `keep`: 1 keeps the image's caption, 0 drops it; some image keeps and some drops. `bucket_rows`: rows in use are the first ones of an image's grid; some image uses all 96 rows.
All inputs are finite; a program needn't handle non-finite values.
Results may differ from a plain program's by a relative error of at most 0.0017.
Values may be sent and summed in bfloat16 or wider, within the bound.
No kernel may reach another device: no remote copies, remote signals or barrier semaphores. Data moves between devices by JAX's collectives and lax.ppermute only.
A program may use at most 128 MiB of HBM per device.

v0:
```python
import jax
import jax.numpy as jnp
from jax import lax
from jax.sharding import PartitionSpec as P

HDIM = 32
norm_eps = 1e-06
attn_eps = 1e-06


def body(tokens, norm_gain, caption, null_caption, keep, bucket_rows, w_qkv):
    grid_rows = tokens.shape[1]
    grid_cols = tokens.shape[2]
    features_count = tokens.shape[3]
    token_count = grid_rows * grid_cols
    features = tokens.reshape(token_count, features_count).astype(jnp.float32)
    mean_square = jnp.mean(features * features, axis=1, keepdims=True)
    condition = jnp.where(keep[0] > 0, caption[0], null_caption).astype(jnp.float32)
    hidden = (
        features * lax.rsqrt(mean_square + norm_eps) * norm_gain.astype(jnp.float32) + condition
    ).astype(jnp.bfloat16)
    rows_whole = lax.all_gather(w_qkv, "img", axis=0, tiled=True)
    projected = jnp.dot(
        hidden,
        lax.all_gather(rows_whole, "seq", axis=1, tiled=True),
        preferred_element_type=jnp.float32,
    )
    inner_width = projected.shape[1] // 3
    head_count = inner_width // HDIM
    grid_row = (
        lax.axis_index("seq") * grid_rows + jnp.arange(token_count, dtype=jnp.int32) // grid_cols
    )
    live_mask = (grid_row < bucket_rows[0]).astype(jnp.float32)
    queries = jax.nn.relu(projected[:, :inner_width]).reshape(token_count, head_count, HDIM)
    keys_relu = jax.nn.relu(projected[:, inner_width : 2 * inner_width]).reshape(
        token_count, head_count, HDIM
    )
    keys_relu = keys_relu * live_mask[:, None, None]
    values = projected[:, 2 * inner_width :].reshape(token_count, head_count, HDIM)
    state_outer = jnp.einsum("thd,the->hde", keys_relu, values, precision=lax.Precision.HIGHEST)
    key_total = jnp.sum(keys_relu, axis=0)
    state_outer, key_total = lax.psum((state_outer, key_total), "seq")
    numerator = jnp.einsum("thd,hde->the", queries, state_outer, precision=lax.Precision.HIGHEST)
    denominator = jnp.einsum("thd,hd->th", queries, key_total, precision=lax.Precision.HIGHEST)
    result = numerator / (denominator[:, :, None] + attn_eps) * live_mask[:, None, None]
    return result.reshape(1, grid_rows, grid_cols, inner_width).astype(jnp.bfloat16)


def solution(mesh):
    in_specs = (
        P("img", "seq", None, None),
        P(),
        P("img", None),
        P(),
        P("img"),
        P("img"),
        P("img", "seq"),
    )
    out_specs = P("img", "seq", None, None)
    return jax.shard_map(body, mesh=mesh, in_specs=in_specs, out_specs=out_specs, check_vma=False)
```

profile of v0, /device:TPU:2, one launch (start us, length us, event | category | flops | bytes accessed | tf_op | source)
XLA Modules:
  0.0 393.1 jit_solution(5974640022013583326)
XLA Ops:
  6.5 27.0 %all-gather = bf16[16,140,108]{2,1,0:T(8,128)(2,1)S(1)} all-gather(bf16[1,140,108]{2,1,0:T(8,128)(2,1)} %bitcast.47), channel_id=1, replica_groups=mesh['seq'=32,'img'=16] {'img'}, dimensions={0}, use_global_device_ids=true | all-gather | bytes 514080 | tf_op jit(solution)/shard_map/all_gather | solution.py:22
  33.6 0.2 reshape.71
  33.8 1.1 copy.18
  35.6 2.6 copy.17
  38.8 0.7 convert_element_type.42
  39.5 1.3 reduce.2
  40.9 1.8 multiply_reduce_fusion
  42.7 0.7 select_convert_fusion
  43.4 1.7 fusion.2
  45.1 95.0 %all-gather.4.cloned.1.call-done = bf16[32,108,2240]{2,1,0:T(8,128)(2,1)} async-done(((bf16[1,108,2240]{2,1,0:T(8,128)(2,1)}), bf16[32,108,2240]{2,1,0:T(8,128)(2,1)}) %all-gather.4.cloned.1.call-update) | async-done | bytes 15482896 | tf_op jit(solution)/shard_map/all_gather | solution.py:25
  140.1 19.5 %reshape.73 = bf16[3456,2240]{1,0:T(8,128)(2,1)} reshape(bf16[32,108,2240]{2,1,0:T(8,128)(2,1)} %all-gather.4.cloned.1.call-done) | data formatting | bytes 30965760
  159.6 10.4 %fusion.17 = f32[384,3456]{1,0:T(8,128)S(1)} fusion(bf16[384,2240]{1,0:T(8,128)(2,1)S(1)} %copy-done, bf16[3456,2240]{1,0:T(8,128)(2,1)} %reshape.73), kind=kOutput, calls=%fused_computation.30 | convolution fusion | flops 5945425920 | bytes 22511616 | tf_op jit(solution)/shard_map/dot_general | solution.py:23
  169.9 2.2 multiply_reduce_fusion.1
  172.1 1.2 copy.19
  173.3 2.2 copy.20
  175.5 3.0 fusion.5
  178.5 2.2 copy.21
  180.7 0.1 reduce_sum.22
  180.8 91.4 %psum.15 = f32[36,32]{1,0:T(8,128)S(1)} all-reduce(f32[36,32]{1,0:T(8,128)S(1)} %reduce_sum.22), channel_id=1, replica_groups=mesh['seq'=32,'img'=16] {'seq'}, use_global_device_ids=true, to_apply=%region_3.4 | all-reduce | flops 1152 | bytes 9216 | tf_op jit(solution)/shard_map/psum | solution.py:42
  272.2 1.1 fusion.9
  273.3 107.9 %all-reduce.2.cloned.1.call-done = f32[36,32,32]{2,1,0:T(8,128)} async-done(((f32[36,32,32]{2,1,0:T(8,128)}), f32[36,32,32]{2,1,0:T(8,128)}) %all-reduce.2.cloned.1.call-update) | async-done | bytes 147472 | tf_op jit(solution)/shard_map/psum | solution.py:42
  381.2 2.8 fusion.4
  384.0 0.3 convert_element_type.47
  384.3 1.9 copy.23
  (9 shorter events, 0.1 us)
Async XLA Ops:
  6.5 133.5 %all-gather.4.cloned.1.call-start = ((), (), s32[]{:S(2)}) async-start(), calls=%async_computation.1 | async-start | bytes 17031168 | tf_op jit(solution)/shard_map/all_gather | solution.py:25
  34.9 346.3 %all-reduce.2.cloned.1.call-start = ((), (), s32[]{:S(2)}) async-start(), calls=%async_computation | async-start | bytes 1179648 | tf_op jit(solution)/shard_map/psum | solution.py:42
  45.1 114.5 %copy-start = (bf16[384,2240]{1,0:T(8,128)(2,1)S(1)}, bf16[384,2240]{1,0:T(8,128)(2,1)}, u32[]{:S(2)}) copy-start(bf16[384,2240]{1,0:T(8,128)(2,1)} %fusion.2) | copy-start | bytes 5160964
Sparse Core Ops, SparseCore 0:
  35.0 105.0 all-gather.3
  178.6 202.5 all-reduce.1
where the time goes:
time: 394 us; the launch traced here: 393 us
  waiting for transfers between devices  203 us (52%)
  blocking collectives  118 us (30%)
  local copies, waits for them, and re-layouts  31.2 us (8%)
  matrix products  17.3 us (4%)
  between operations  14.8 us (4%)
  other arithmetic  8.47 us (2%)
    psum x1, waiting for transfers between devices, body(): state_outer, key_total = lax.psum((state_outer, key_total), 'seq')  108 us
    all_gather x1, waiting for transfers between devices, body(): lax.all_gather(rows_whole, 'seq', axis=1, tiled=True)  95 us
    psum x1, blocking collectives, body(): state_outer, key_total = lax.psum((state_outer, key_total), 'seq')  91.4 us
    all_gather x1, blocking collectives, body(): rows_whole = lax.all_gather(w_qkv, 'img', axis=0, tiled=True)  27 us
    unnamed x5, local copies, waits for them, and re-layouts  20.8 us
    dot_general x1, matrix products, body(): jnp.dot(hidden, lax.all_gather(rows_whole, 'seq', axis=1, tiled=True), pr...  10.4 us
  transfers between devices with their start and end apart: 2, of which 2 were waited for; matrix products, arithmetic and copies ran while one was open for 3% of the time, Pallas kernels for 0%

commit v1 on v0

--- a/solution.py
+++ b/solution.py
@@ -22,7 +22,9 @@
     rows_whole = lax.all_gather(w_qkv, "img", axis=0, tiled=True)
     projected = jnp.dot(
         hidden,
-        lax.all_gather(rows_whole, "seq", axis=1, tiled=True),
+        jnp.concatenate(
+            lax.all_to_all(jnp.stack([rows_whole] * lax.axis_size("seq")), "seq", 0, 0), axis=1
+        ),
         preferred_element_type=jnp.float32,
     )
     inner_width = projected.shape[1] // 3

time: 394 us -> 1020 us (2.59)
  waiting for transfers between devices: 203 us -> 803 us
  starting transfers between devices: 0.04 us -> 12.9 us
  blocking collectives: 118 us -> 129 us
    all_to_all x0 -> x1, waiting for transfers between devices: none -> 700 us  [body(): lax.all_to_all(jnp.stack([rows_whole] * lax.axis_size('seq')), 'seq', 0, 0)]
    all_gather x1 -> x0, waiting for transfers between devices: 95 us -> none  [body(): lax.all_gather(rows_whole, 'seq', axis=1, tiled=True)]
    unnamed x5 -> x12, local copies, waits for them, and re-layouts: 20.8 us -> 0.5 us
    reshape x0 -> x1, local copies, waits for them, and re-layouts: none -> 19.6 us  [body(): jnp.concatenate(lax.all_to_all(jnp.stack([rows_whole] * lax.axis_size('se...]
    all_to_all x0 -> x1, starting transfers between devices: none -> 12.8 us  [body(): lax.all_to_all(jnp.stack([rows_whole] * lax.axis_size('seq')), 'seq', 0, 0)]
    psum x1, blocking collectives: 91.4 us -> 102 us  [body(): state_outer, key_total = lax.psum((state_outer, key_total), 'seq')]
  transfers between devices with their start and end apart: 2 -> 2, of which waited for: 2 -> 2; matrix products, arithmetic and copies ran while one was open for 3% -> 1% of each run, Pallas kernels for 0% -> 0%
where the time goes in v1:
time: 1020 us
  waiting for transfers between devices  803 us (79%)
  blocking collectives  129 us (13%)
  local copies, waits for them, and re-layouts  36.1 us (4%)
  matrix products  17.3 us (2%)
  between operations  14.8 us (1%)
  starting transfers between devices  12.9 us (1%)
    all_to_all x1, waiting for transfers between devices, body(): lax.all_to_all(jnp.stack([rows_whole] * lax.axis_size('seq')), 'seq', 0, 0)  700 us
    psum x1, waiting for transfers between devices, body(): state_outer, key_total = lax.psum((state_outer, key_total), 'seq')  103 us
    psum x1, blocking collectives, body(): state_outer, key_total = lax.psum((state_outer, key_total), 'seq')  102 us
    all_gather x1, blocking collectives, body(): rows_whole = lax.all_gather(w_qkv, 'img', axis=0, tiled=True)  27 us
  transfers between devices with their start and end apart: 2, of which 2 were waited for; matrix products, arithmetic and copies ran while one was open for 1% of the time, Pallas kernels for 0%

profile of v1, /device:TPU:2, one launch (start us, length us, event | category | flops | bytes accessed | tf_op | source)
XLA Modules:
  0.0 1016.9 jit_solution(13085250895373773123)
XLA Ops:
  6.5 27.0 %all-gather = bf16[16,140,108]{2,1,0:T(8,128)(2,1)S(1)} all-gather(bf16[1,140,108]{2,1,0:T(8,128)(2,1)} %bitcast.38), channel_id=1, replica_groups=mesh['seq'=32,'img'=16] {'img'}, dimensions={0}, use_global_device_ids=true | all-gather | bytes 514080 | tf_op jit(solution)/shard_map/all_gather | solution.py:22
  33.6 0.2 reshape.90
  33.8 0.3 copy.18
  34.1 5.9 stack.2
  39.9 12.8 %all-to-all-start = ((bf16[32,2240,108]{1,2,0:T(8,128)(2,1)}), bf16[32,2240,108]{1,2,0:T(8,128)(2,1)}, u32[]{:S(2)}, u32[]{:S(2)}) async-start(bf16[32,2240,108]{1,2,0:T(8,128)(2,1)} %stack.2), calls=%async_computation | async-start | bytes 33030144 | tf_op jit(solution)/shard_map/all_to_all | solution.py:26
  52.8 0.0 all-reduce.2.cloned.1.call-start
  54.2 0.3 fusion
  54.6 1.3 fusion.3
  55.9 2.2 copy.17
  58.2 700.0 %all-to-all-done = bf16[32,2240,108]{1,2,0:T(8,128)(2,1)} async-done(((bf16[32,2240,108]{1,2,0:T(8,128)(2,1)}), bf16[32,2240,108]{1,2,0:T(8,128)(2,1)}, u32[]{:S(2)}, u32[]{:S(2)}) %all-to-all-start) | async-done | bytes 15482912 | tf_op jit(solution)/shard_map/all_to_all | solution.py:26
  758.2 19.6 %reshape.85 = bf16[2240,3456]{0,1:T(8,128)(2,1)} reshape(bf16[2240,32,108]{0,2,1:T(8,128)(2,1)} %bitcast.3) | data formatting | bytes 30965760 | tf_op jit(solution)/shard_map/reshape | solution.py:25
  777.8 10.4 %fusion.18 = f32[384,3456]{1,0:T(8,128)S(1)} fusion(bf16[384,2240]{1,0:T(8,128)(2,1)S(1)} %bitcast.36, bf16[2240,3456]{0,1:T(8,128)(2,1)} %reshape.85), kind=kOutput, calls=%fused_computation.31 | convolution fusion | flops 5945425920 | bytes 22511616 | tf_op jit(solution)/shard_map/dot_general | solution.py:23
  788.1 2.2 multiply_reduce_fusion
  790.3 1.2 copy.19
  791.5 2.2 copy.20
  793.7 3.0 fusion.6
  796.7 2.2 copy.21
  798.9 0.1 reduce_sum.22
  799.0 101.6 %psum.15 = f32[36,32]{1,0:T(8,128)S(1)} all-reduce(f32[36,32]{1,0:T(8,128)S(1)} %reduce_sum.22), channel_id=1, replica_groups=mesh['seq'=32,'img'=16] {'seq'}, use_global_device_ids=true, to_apply=%region_3.4 | all-reduce | flops 1152 | bytes 9216 | tf_op jit(solution)/shard_map/psum | solution.py:44
  900.6 1.1 fusion.10
  901.7 103.2 %all-reduce.2.cloned.1.call-done = f32[36,32,32]{2,1,0:T(8,128)} async-done(((f32[36,32,32]{2,1,0:T(8,128)}), f32[36,32,32]{2,1,0:T(8,128)}) %all-reduce.2.cloned.1.call-update) | async-done | bytes 147472 | tf_op jit(solution)/shard_map/psum | solution.py:44
  1005.0 2.8 fusion.5
  1007.8 0.3 convert_element_type.45
  1008.1 1.9 copy.23
  (17 shorter events, 0.1 us)
Async XLA Ops:
  39.9 14.2 %copy-start.3 = (bf16[2240]{0:T(1024)(128)(2,1)S(1)}, bf16[2240]{0:T(1024)(128)(2,1)}, u32[]{:S(2)}) copy-start(bf16[2240]{0:T(1024)(128)(2,1)} %param.8) | copy-start | bytes 13444
  39.9 14.2 %copy-start.2 = (bf16[1,2240]{1,0:T(2,128)(2,1)S(1)}, bf16[1,2240]{1,0:T(2,128)(2,1)}, u32[]{:S(2)}) copy-start(bf16[1,2240]{1,0:T(2,128)(2,1)} %param.9) | copy-start | bytes 13444
  39.9 14.3 %copy-start = (bf16[1,3,128,2240]{2,3,1,0:T(8,128)(2,1)S(1)}, bf16[1,3,128,2240]{2,3,1,0:T(8,128)(2,1)}, u32[]{:S(2)}) copy-start(bf16[1,3,128,2240]{2,3,1,0:T(8,128)(2,1)} %param.7) | copy-start | bytes 5160964
  39.9 718.2 %all-to-all-start = ((bf16[32,2240,108]{1,2,0:T(8,128)(2,1)}), bf16[32,2240,108]{1,2,0:T(8,128)(2,1)}, u32[]{:S(2)}, u32[]{:S(2)}) async-start(bf16[32,2240,108]{1,2,0:T(8,128)(2,1)} %stack.2), calls=%async_computation | async-start | bytes 33030144 | tf_op jit(solution)/shard_map/all_to_all | solution.py:26
  52.8 1.8 copy-start.4
  52.8 952.2 %all-reduce.2.cloned.1.call-start = ((), (), s32[]{:S(2)}) async-start(), calls=%async_computation.1 | async-start | bytes 1179648 | tf_op jit(solution)/shard_map/psum | solution.py:44
  758.2 19.6 %copy-start.1 = (bf16[1,3,128,2240]{3,2,1,0:T(8,128)(2,1)S(1)}, bf16[1,3,128,2240]{3,2,1,0:T(8,128)(2,1)}, u32[]{:S(2)}) copy-start(bf16[1,3,128,2240]{3,2,1,0:T(8,128)(2,1)} %copy.17) | copy-start | bytes 5160964
Sparse Core Ops, SparseCore 0:
  796.9 208.0 all-reduce.1
